TPU v7x, 256 devices: a whole 4x4x8 slice. The times are simulated.
256 devices in a mesh: gx: 32 (over z, x), gy: 4 (over y), gz: 2 (over core).
Axes of the slice: x: 4, y: 4, z: 8, core: 2. Of those that a mesh axis runs over, the one named last changes fastest.
Arguments:
- viscosity: bfloat16 [8, 2048, 1024], P('gz', 'gx', 'gy'), may hold values from 0.29882812 to 3
- velocity: bfloat16 [2, 8, 2048, 1024], P(None, 'gz', 'gx', 'gy'), may hold values from -6 to 6
- log_friction: float32 [2048, 1024], P('gx', 'gy'), may hold values from -1 to 1
- step_dir: float32 [2048, 1024], P('gx', 'gy'), may hold values from -6 to 6
- obs_weight: float32 [2048, 1024], P('gx', 'gy'), may hold values from 1 to 8
- tile_mask: int32 [32, 16], P('gx', 'gy'), may hold values from 0 to 2
- contact: int32 [2048, 1024], P('gx', 'gy'), may hold values 0 or 1
Outputs:
- depth_response: float32 [2, 2048, 1024], P(None, 'gx', 'gy')
- hess_vec: float32 [2048, 1024], P('gx', ('gy', 'gz'))
Inputs may be any that keep to these rules, and one draw needn't show every extreme that they name: `tile_mask`: each tile's class: 0 ocean, 1 floating ice, 2 grounded ice.
All inputs are finite; a program needn't handle non-finite values. No bound on the sum of `contact` on one device may be relied on, other than what follows from the above.
Results may differ from a plain program's by a relative error of at most 0.0024.
Values may be sent and summed in bfloat16 or wider, within the bound.
A program may use at most 64 MiB of HBM per device.

v0:
```python
import jax
import jax.numpy as jnp
from jax import lax
from jax.sharding import PartitionSpec as P

ITERS = 8
SWEEPS = 2
TILE = 64
ASPECT = 16.0
LOWER = 0.1
UPPER = 2.0


def extended(cells, sides, width):
    for axis, dim in sides:
        count = lax.axis_size(axis)
        ends = count - 1
        head = lax.slice_in_dim(cells, 0, width, axis=dim)
        tail = lax.slice_in_dim(cells, cells.shape[dim] - width, cells.shape[dim], axis=dim)
        cells = jnp.concatenate(
            [
                lax.ppermute(tail, axis, [(i, (i + 1) % count) for i in range(ends)]),
                cells,
                lax.ppermute(head, axis, [((i + 1) % count, i) for i in range(ends)]),
            ],
            axis=dim,
        )
    return cells


def shifted_2(value, axis, by):
    size = lax.axis_size(axis)
    pairs = [(i, i + by) for i in range(size) if 0 <= i + by < size]
    return lax.ppermute(value, axis, pairs)


def expand(tiles):
    return jnp.repeat(jnp.repeat(tiles, TILE, axis=0), TILE, axis=1)


def coefficients(values):
    center_eta = values[1:-1, 1:-1, 1:-1]

    def flat(beside):
        return jnp.where(beside > 0, 0.5 * (center_eta + beside), center_eta)

    def vertical(beside):
        return jnp.where(
            beside > 0, ASPECT * 0.5 * (center_eta + beside), jnp.zeros_like(center_eta)
        )

    return (
        flat(values[1:-1, :-2, 1:-1]),
        flat(values[1:-1, 2:, 1:-1]),
        flat(values[1:-1, 1:-1, :-2]),
        flat(values[1:-1, 1:-1, 2:]),
        vertical(values[:-2, 1:-1, 1:-1]),
        vertical(values[2:, 1:-1, 1:-1]),
    )


def stencil(padded, face_terms, diagonal, ice_cells):
    shifted_all = (
        padded[:, 1:-1, :-2, 1:-1],
        padded[:, 1:-1, 2:, 1:-1],
        padded[:, 1:-1, 1:-1, :-2],
        padded[:, 1:-1, 1:-1, 2:],
        padded[:, :-2, 1:-1, 1:-1],
        padded[:, 2:, 1:-1, 1:-1],
    )
    beside = face_terms[0] * shifted_all[0].astype(jnp.float32)
    for factor, shifted in zip(face_terms[1:], shifted_all[1:]):
        beside = beside + factor * shifted.astype(jnp.float32)
    center = padded[:, 1:-1, 1:-1, 1:-1].astype(jnp.float32)
    return ice_cells * (diagonal * center - beside) + (1.0 - ice_cells) * center


def chebyshev(operator, inverse_diag, forcing):
    centre_value = (UPPER + LOWER) / 2.0
    half_width = (UPPER - LOWER) / 2.0
    sigma_ratio = centre_value / half_width
    solution = jnp.zeros(forcing.shape, jnp.float32)
    for sweep_index in range(SWEEPS):
        if sweep_index == 0:
            residual = forcing
        else:
            residual = forcing - operator(solution.astype(jnp.bfloat16))
        direction = inverse_diag * residual / centre_value
        rho_now = 1.0 / sigma_ratio
        for iter_index in range(ITERS):
            solution = solution + direction
            if iter_index + 1 < ITERS:
                residual = residual - operator(direction.astype(jnp.bfloat16))
                rho_next = 1.0 / (2.0 * sigma_ratio - rho_now)
                direction = (
                    rho_next * rho_now * direction
                    + 2.0 * rho_next / half_width * inverse_diag * residual
                )
                rho_now = rho_next
    return solution


def per_device(viscosity, velocity, log_friction, step_dir, obs_weight, tile_mask, contact):
    ice_cells = expand(tile_mask > 0).astype(jnp.float32)
    grounded = expand(tile_mask == 2).astype(jnp.float32)
    friction = jnp.exp(log_friction) * grounded * contact.astype(jnp.float32)
    half_cols = log_friction.shape[1] // 2
    stacked = viscosity[None]

    def with_rims(field):
        return extended(field, (("gx", 2), ("gy", 3), ("gz", 1)), 1)

    layers = stacked.shape[1]
    lowest = jnp.logical_and(jnp.arange(layers) == 0, lax.axis_index("gz") == 0)
    bottom = lowest.astype(jnp.float32)[:, None, None]
    values = with_rims(stacked)[0].astype(jnp.float32)
    face_terms = coefficients(values)
    diagonal = (
        face_terms[0]
        + face_terms[1]
        + face_terms[2]
        + face_terms[3]
        + face_terms[4]
        + face_terms[5]
        + friction * bottom
    )
    inverse_diag = ice_cells / diagonal + (1.0 - ice_cells)

    def operator(field):
        return stencil(with_rims(field), face_terms, diagonal, ice_cells)

    u_base = velocity[:, 0].astype(jnp.float32)
    forcing = (-(friction * step_dir) * u_base)[:, None] * bottom
    response = chebyshev(operator, inverse_diag, forcing)
    column_sum = jnp.sum(response, axis=1)
    depth_local = lax.psum(column_sum, "gz")
    adjoint_rhs = jnp.broadcast_to((ice_cells * obs_weight * depth_local)[:, None], response.shape)
    multiplier = chebyshev(operator, inverse_diag, adjoint_rhs)
    basal = -friction * jnp.sum(u_base * multiplier[:, 0], axis=0)
    upper_half = shifted_2(basal[:, half_cols:], "gz", 1)
    hess_vec = jnp.where(lax.axis_index("gz") == 0, basal[:, :half_cols], upper_half)
    return (depth_local, hess_vec)


def solution(mesh):
    in_specs = (
        P("gz", "gx", "gy"),
        P(None, "gz", "gx", "gy"),
        P("gx", "gy"),
        P("gx", "gy"),
        P("gx", "gy"),
        P("gx", "gy"),
        P("gx", "gy"),
    )
    out_specs = (P(None, "gx", "gy"), P("gx", ("gy", "gz")))
    return jax.shard_map(
        per_device, mesh=mesh, in_specs=in_specs, out_specs=out_specs, check_vma=False
    )
```

profile of v0, /device:TPU:103, one launch (start us, length us, event | category | flops | bytes accessed | tf_op | source)
XLA Modules:
  0.0 866.0 jit_solution(4809203129304106115)
XLA Ops:
  8.0 4.7 collective-permute-start
  30.2 5.4 collective-permute-start.5
  44.0 4.7 collective-permute-done.7
  59.5 5.1 collective-permute-start.11
  71.9 4.3 collective-permute-done.13
  86.8 4.9 collective-permute-start.17
  99.0 4.3 collective-permute-done.19
  112.6 4.9 collective-permute-start.23
  124.8 4.3 collective-permute-done.25
  138.4 4.9 collective-permute-start.29
  150.6 4.3 collective-permute-done.31
  164.2 4.9 collective-permute-start.35
  189.9 4.9 collective-permute-start.41
  202.1 4.3 collective-permute-done.43
  215.7 4.9 collective-permute-start.47
  229.1 4.3 collective-permute-done.49
  242.7 4.9 collective-permute-start.53
  254.9 4.3 collective-permute-done.55
  268.4 4.9 collective-permute-start.59
  280.6 4.3 collective-permute-done.61
  294.2 4.9 collective-permute-start.65
  306.4 4.3 collective-permute-done.67
  319.9 4.9 collective-permute-start.71
  345.7 4.9 collective-permute-start.77
  357.9 4.3 collective-permute-done.79
  371.5 4.9 collective-permute-start.83
  397.3 4.9 collective-permute-start.89
  409.5 4.3 collective-permute-done.91
  423.0 4.9 collective-permute-start.95
  432.7 24.6 %all-reduce.2.cloned.1.call-done = f32[2,64,256]{2,1,0:T(8,128)} async-done(((f32[2,64,256]{2,1,0:T(8,128)}), f32[2,64,256]{2,1,0:T(8,128)}) %all-reduce.2.cloned.1.call-update) | async-done | bytes 131088 | tf_op jit(solution)/shard_map/psum | solution.py:136
  458.2 4.4 collective-permute-start.96
  464.5 5.8 collective-permute-done.97
  481.0 5.0 collective-permute-start.101
  493.3 4.3 collective-permute-done.103
  508.5 4.9 collective-permute-start.107
  535.5 4.9 collective-permute-start.113
  561.3 4.9 collective-permute-start.119
  587.1 4.9 collective-permute-start.125
  612.8 4.9 collective-permute-start.131
  638.7 4.9 collective-permute-start.137
  665.9 4.9 collective-permute-start.143
  691.9 4.9 collective-permute-start.149
  717.7 4.9 collective-permute-start.155
  743.5 4.9 collective-permute-start.161
  769.2 4.9 collective-permute-start.167
  795.0 4.9 collective-permute-start.173
  820.7 4.9 collective-permute-start.179
  846.5 4.9 collective-permute-start.185
  (527 shorter events, 601.3 us)
Async XLA Ops:
  7.2 450.0 %all-reduce.2.cloned.1.call-start = ((), (), s32[]{:S(2)}) async-start(), calls=%async_computation | async-start | bytes 262144 | tf_op jit(solution)/shard_map/psum | solution.py:136
  8.0 8.8 %collective-permute-start = (bf16[1,4,1,256]{3,2,1,0:T(2,128)(2,1)S(1)}, bf16[1,4,1,256]{3,2,1,0:T(2,128)(2,1)S(1)}, u32[]{:S(2)}, u32[]{:S(2)}) collective-permute-start(bf16[1,4,1,256]{3,2,1,0:T(2,128)(2,1)S(1)} %get-tuple-element.274), channel_id=1, source_target_pairs={{0,8},{8,16},{16,24},{24,32},{32,40},{40,48},{48,56},{56,64},{64,7... | collective-permute-start | bytes 6152 | tf_op jit(solution)/shard_map/ppermute | solution.py:22
  12.7 7.7 collective-permute-start.1
  28.9 6.8 collective-permute-start.4
  30.2 6.3 collective-permute-start.5
  40.9 7.7 collective-permute-start.7
  58.2 6.4 collective-permute-start.10
  68.6 7.7 collective-permute-start.13
  85.5 6.2 collective-permute-start.16
  95.7 7.7 collective-permute-start.19
  111.3 6.2 collective-permute-start.22
  121.4 7.7 collective-permute-start.25
  137.1 6.2 collective-permute-start.28
  147.2 7.7 collective-permute-start.31
  162.9 6.2 collective-permute-start.34
  173.0 7.7 collective-permute-start.37
  188.6 6.2 collective-permute-start.40
  198.8 7.7 collective-permute-start.43
  214.4 6.2 collective-permute-start.46
  225.7 7.7 collective-permute-start.49
  251.5 7.7 collective-permute-start.55
  267.1 6.2 collective-permute-start.58
  277.3 7.7 collective-permute-start.61
  303.0 7.7 collective-permute-start.67
  328.8 7.7 collective-permute-start.73
  344.4 6.2 collective-permute-start.76
  354.5 7.7 collective-permute-start.79
  380.3 7.7 collective-permute-start.85
  406.1 7.7 collective-permute-start.91
  458.2 6.3 collective-permute-start.96
  462.6 7.7 collective-permute-start.97
  479.7 6.3 collective-permute-start.100
  490.0 7.7 collective-permute-start.103
  517.4 7.7 collective-permute-start.109
  544.3 7.7 collective-permute-start.115
  570.1 7.7 collective-permute-start.121
  595.9 7.7 collective-permute-start.127
  621.7 7.7 collective-permute-start.133
  649.0 7.7 collective-permute-start.139
  674.7 7.7 collective-permute-start.145
  690.4 6.4 collective-permute-start.148
  700.8 7.7 collective-permute-start.151
  726.5 7.7 collective-permute-start.157
  752.3 7.7 collective-permute-start.163
  778.0 7.7 collective-permute-start.169
  803.8 7.7 collective-permute-start.175
  829.5 7.7 collective-permute-start.181
  845.2 6.2 collective-permute-start.184
  (150 other events, 1594.3 us)
Sparse Core Ops, SparseCore 0:
  432.0 25.2 all-reduce.1
where the time goes:
time: 880 us; the launch traced here: 866 us
  starting transfers between devices  460 us (52%)
  waiting for transfers between devices  331 us (38%)
  other arithmetic  51.4 us (6%)
  between operations  17.1 us (2%)
    ppermute x93, starting transfers between devices, extended(): lax.ppermute(head, axis, [((i + 1) % count, i) for i in range(ends)])  294 us
    ppermute x93, waiting for transfers between devices, extended(): lax.ppermute(head, axis, [((i + 1) % count, i) for i in range(ends)])  282 us
    ppermute x93, starting transfers between devices, extended(): lax.ppermute(tail, axis, [(i, (i + 1) % count) for i in range(ends)])  165 us
    convert_element_type x27, other arithmetic, chebyshev(): residual = residual - operator(direction.astype(jnp.bfloat16))  26 us
    psum x1, waiting for transfers between devices, per_device(): depth_local = lax.psum(column_sum, 'gz')  24.6 us
    ppermute x93, waiting for transfers between devices, extended(): lax.ppermute(tail, axis, [(i, (i + 1) % count) for i in range(ends)])  22.6 us
  transfers between devices with their start and end apart: 188, of which 126 were waited for; matrix products, arithmetic and copies ran while one was open for 0% of the time, Pallas kernels for 0%

commit v1 on v0

--- a/solution.py
+++ b/solution.py
@@ -133,7 +133,7 @@
     forcing = (-(friction * step_dir) * u_base)[:, None] * bottom
     response = chebyshev(operator, inverse_diag, forcing)
     column_sum = jnp.sum(response, axis=1)
-    depth_local = lax.psum(column_sum, "gz")
+    depth_local = jnp.sum(lax.all_gather(column_sum, "gz"), axis=0)
     adjoint_rhs = jnp.broadcast_to((ice_cells * obs_weight * depth_local)[:, None], response.shape)
     multiplier = chebyshev(operator, inverse_diag, adjoint_rhs)
     basal = -friction * jnp.sum(u_base * multiplier[:, 0], axis=0)

time: 880 us -> 835 us (0.949)
  waiting for transfers between devices: 331 us -> 305 us
  between operations: 17.1 us -> 3.76 us
    psum x1 -> x0, waiting for transfers between devices: 24.6 us -> none  [per_device(): depth_local = lax.psum(column_sum, 'gz')]
  transfers between devices with their start and end apart: 188 -> 187, of which waited for: 126 -> 125; matrix products, arithmetic and copies ran while one was open for 0% -> 0% of each run, Pallas kernels for 0% -> 0%
where the time goes in v1:
time: 835 us; the launch traced here: 822 us
  starting transfers between devices  454 us (54%)
  waiting for transfers between devices  305 us (37%)
  other arithmetic  51.2 us (6%)
    ppermute x93, starting transfers between devices, extended(): lax.ppermute(head, axis, [((i + 1) % count, i) for i in range(ends)])  295 us
    ppermute x93, waiting for transfers between devices, extended(): lax.ppermute(head, axis, [((i + 1) % count, i) for i in range(ends)])  280 us
    ppermute x93, starting transfers between devices, extended(): lax.ppermute(tail, axis, [(i, (i + 1) % count) for i in range(ends)])  159 us
    convert_element_type x27, other arithmetic, chebyshev(): residual = residual - operator(direction.astype(jnp.bfloat16))  25.2 us
    ppermute x93, waiting for transfers between devices, extended(): lax.ppermute(tail, axis, [(i, (i + 1) % count) for i in range(ends)])  23.1 us
  transfers between devices with their start and end apart: 187, of which 125 were waited for; matrix products, arithmetic and copies ran while one was open for 0% of the time, Pallas kernels for 0%

profile of v1, /device:TPU:103, one launch (start us, length us, event | category | flops | bytes accessed | tf_op | source)
XLA Modules:
  0.0 821.7 jit_solution(7901854004900305873)
XLA Ops:
  1.4 4.7 collective-permute-start
  23.6 5.4 collective-permute-start.5
  37.4 4.7 collective-permute-done.7
  52.9 5.1 collective-permute-start.11
  65.3 4.3 collective-permute-done.13
  80.2 4.9 collective-permute-start.17
  92.4 4.3 collective-permute-done.19
  105.9 4.9 collective-permute-start.23
  118.1 4.3 collective-permute-done.25
  131.7 4.9 collective-permute-start.29
  143.9 4.3 collective-permute-done.31
  157.4 4.9 collective-permute-start.35
  169.6 4.3 collective-permute-done.37
  183.3 4.9 collective-permute-start.41
  209.1 4.9 collective-permute-start.47
  222.5 4.3 collective-permute-done.49
  236.0 4.9 collective-permute-start.53
  248.2 4.3 collective-permute-done.55
  261.7 4.9 collective-permute-start.59
  273.9 4.3 collective-permute-done.61
  287.5 4.9 collective-permute-start.65
  313.2 4.9 collective-permute-start.71
  325.4 4.3 collective-permute-done.73
  339.4 4.9 collective-permute-start.77
  351.5 4.3 collective-permute-done.79
  365.1 4.9 collective-permute-start.83
  377.3 4.3 collective-permute-done.85
  390.8 4.9 collective-permute-start.89
  403.0 4.3 collective-permute-done.91
  416.7 4.9 collective-permute-start.95
  434.2 4.3 collective-permute-done.97
  447.7 4.9 collective-permute-start.101
  459.9 4.3 collective-permute-done.103
  473.6 4.9 collective-permute-start.107
  499.4 5.0 collective-permute-start.113
  511.7 4.3 collective-permute-done.115
  525.3 4.9 collective-permute-start.119
  551.0 4.9 collective-permute-start.125
  576.8 4.9 collective-permute-start.131
  602.6 4.9 collective-permute-start.137
  629.8 4.9 collective-permute-start.143
  655.5 5.1 collective-permute-start.149
  681.3 4.9 collective-permute-start.155
  707.0 4.9 collective-permute-start.161
  732.7 4.9 collective-permute-start.167
  758.4 4.9 collective-permute-start.173
  784.1 4.9 collective-permute-start.179
  809.9 4.9 collective-permute-start.185
  (525 shorter events, 591.8 us)
Async XLA Ops:
  1.4 8.8 %collective-permute-start = (bf16[1,4,1,256]{3,2,1,0:T(2,128)(2,1)S(1)}, bf16[1,4,1,256]{3,2,1,0:T(2,128)(2,1)S(1)}, u32[]{:S(2)}, u32[]{:S(2)}) collective-permute-start(bf16[1,4,1,256]{3,2,1,0:T(2,128)(2,1)S(1)} %get-tuple-element.274), channel_id=1, source_target_pairs={{0,8},{8,16},{16,24},{24,32},{32,40},{40,48},{48,56},{56,64},{64,7... | collective-permute-start | bytes 6152 | tf_op jit(solution)/shard_map/ppermute | solution.py:22
  6.1 7.7 collective-permute-start.1
  22.3 6.8 collective-permute-start.4
  23.6 6.3 collective-permute-start.5
  34.4 7.7 collective-permute-start.7
  51.6 6.4 collective-permute-start.10
  61.9 7.7 collective-permute-start.13
  78.9 6.2 collective-permute-start.16
  89.0 7.7 collective-permute-start.19
  104.6 6.2 collective-permute-start.22
  114.7 7.7 collective-permute-start.25
  130.4 6.2 collective-permute-start.28
  140.5 7.7 collective-permute-start.31
  156.1 6.2 collective-permute-start.34
  166.2 7.7 collective-permute-start.37
  182.0 6.2 collective-permute-start.40
  192.2 7.7 collective-permute-start.43
  219.1 7.7 collective-permute-start.49
  234.7 6.2 collective-permute-start.52
  244.8 7.7 collective-permute-start.55
  260.4 6.2 collective-permute-start.58
  270.5 7.7 collective-permute-start.61
  286.2 6.2 collective-permute-start.64
  296.2 7.7 collective-permute-start.67
  322.0 7.7 collective-permute-start.73
  337.7 6.6 collective-permute-start.76
  348.1 7.7 collective-permute-start.79
  373.9 7.7 collective-permute-start.85
  399.6 7.7 collective-permute-start.91
  415.4 6.8 collective-permute-start.94
  430.8 7.7 collective-permute-start.97
  456.5 7.7 collective-permute-start.103
  482.4 7.7 collective-permute-start.109
  498.1 6.3 collective-permute-start.112
  508.3 7.7 collective-permute-start.115
  534.1 7.7 collective-permute-start.121
  559.8 7.7 collective-permute-start.127
  585.6 7.7 collective-permute-start.133
  612.8 7.7 collective-permute-start.139
  638.5 7.7 collective-permute-start.145
  654.2 6.4 collective-permute-start.148
  664.3 7.7 collective-permute-start.151
  690.0 7.7 collective-permute-start.157
  715.8 7.7 collective-permute-start.163
  741.5 7.7 collective-permute-start.169
  767.2 7.7 collective-permute-start.175
  792.9 7.7 collective-permute-start.181
  808.6 6.2 collective-permute-start.184
  (149 other events, 1592.2 us)
